TPU v7x, 32 devices: a whole 2x2x4 slice. The times are simulated.
32 devices in a mesh: ia: 4 (over z), ja: 4 (over x, core), ka: 2 (over y).
Axes of the slice: x: 2, y: 2, z: 4, core: 2. Of those that a mesh axis runs over, the one named last changes fastest.
Arguments:
- tensor: bfloat16 [64, 256, 512], P('ka', 'ia', 'ja'), may hold values from -768 to 768
- observed: int32 [64, 256, 512], P('ka', 'ia', 'ja'), may hold values from 0 to 1, as said below
- factor_a: bfloat16 [256, 128], P('ia', ('ja', 'ka')), may hold values from -6 to 6
- factor_b: bfloat16 [512, 128], P('ja', ('ia', 'ka')), may hold values from -6 to 6
- factor_c: bfloat16 [64, 128], P('ka', ('ia', 'ja')), may hold values from -6 to 6
Outputs:
- step_a: float32 [256, 128], P('ia', ('ja', 'ka'))
- step_b: float32 [512, 128], P('ja', ('ia', 'ka'))
- step_c: float32 [64, 128], P('ka', ('ia', 'ja'))
Inputs may be any that keep to these rules, and one draw needn't show every extreme that they name: `observed`: a 0/1 weight per cell.
All inputs are finite; a program needn't handle non-finite values.
Results may differ from a plain program's by a relative error of at most 0.0095.
Values may be sent and summed in bfloat16 or wider, within the bound.
A program may use at most 64 MiB of HBM per device.

v0:
```python
import jax
import jax.numpy as jnp
from jax import lax
from jax.sharding import PartitionSpec as P

ITERS = 2
DAMP = 1.0


def against(left_side, right_side):
    return lax.dot_general(
        left_side, right_side, (((1,), (1,)), ((), ())), preferred_element_type=jnp.float32
    )


def local(tensor, observed, factor_a, factor_b, factor_c):
    depth_rows, height_rows, width_cols = tensor.shape
    divisor = width_cols * lax.axis_size("ja") * (depth_rows * lax.axis_size("ka")) / 32.0
    full_a = lax.all_gather(factor_a, ("ja", "ka"), axis=1, tiled=True)
    full_b = lax.all_gather(factor_b, ("ia", "ka"), axis=1, tiled=True)
    full_c = lax.all_gather(factor_c, ("ia", "ja"), axis=1, tiled=True)
    columns = full_a.shape[1]
    wide_a = full_a.astype(jnp.float32)
    wide_c = full_c.astype(jnp.float32)
    weight = (observed.astype(jnp.float32) * (1.0 / divisor)).astype(jnp.bfloat16)
    weight = weight.reshape(depth_rows * height_rows, width_cols)
    paired = (
        (wide_c[:, None, :] * wide_a[None, :, :])
        .astype(jnp.bfloat16)
        .reshape(depth_rows * height_rows, columns)
    )

    def partials(weighted):
        part_b = lax.dot_general(
            weighted, paired, (((0,), (0,)), ((), ())), preferred_element_type=jnp.float32
        )
        mixture = jnp.dot(weighted, full_b, preferred_element_type=jnp.float32).reshape(
            depth_rows, height_rows, columns
        )
        part_a = jnp.einsum("kir,kr->ir", mixture, wide_c)
        part_c = jnp.einsum("kir,ir->kr", mixture, wide_a)
        return (part_a, part_b, part_c)

    def settle(parts):
        total_a = lax.psum(parts[0], ("ja", "ka"))
        total_b = lax.psum(parts[1], ("ia", "ka"))
        total_c = lax.psum(parts[2], ("ia", "ja"))
        return (total_a, total_b, total_c)

    scales = (
        1.0 / lax.axis_size(("ja", "ka")),
        1.0 / lax.axis_size(("ia", "ka")),
        1.0 / lax.axis_size(("ia", "ja")),
    )

    def inner_sum(first, second):
        local_sum = sum(
            (
                jnp.sum(left_side * right_side) * factor
                for left_side, right_side, factor in zip(first, second, scales)
            )
        )
        return lax.psum(local_sum, ("ia", "ja", "ka"))

    def expand(direction):
        hat_a = direction[0].astype(jnp.bfloat16)
        hat_b = direction[1].astype(jnp.bfloat16)
        hat_c = direction[2].astype(jnp.bfloat16)
        return (hat_a, hat_b, hat_c)

    def hessian_times(direction):
        hat_a, hat_b, hat_c = expand(direction)
        sideways = (
            hat_c.astype(jnp.float32)[:, None, :] * wide_a[None, :, :]
            + wide_c[:, None, :] * hat_a.astype(jnp.float32)[None, :, :]
        )
        sideways = sideways.astype(jnp.bfloat16).reshape(depth_rows * height_rows, columns)
        tangent = against(paired, hat_b) + against(sideways, full_b)
        weighted = (weight.astype(jnp.float32) * tangent).astype(jnp.bfloat16)
        parts = settle(partials(weighted))
        return tuple((part + DAMP * vector for part, vector in zip(parts, direction)))

    fitted = against(paired, full_b)
    values = tensor.reshape(depth_rows * height_rows, width_cols).astype(jnp.float32)
    errors = (weight.astype(jnp.float32) * (values - fitted)).astype(jnp.bfloat16)
    gradient = settle(partials(errors))
    solution = tuple((jnp.zeros_like(vector) for vector in gradient))
    residual = gradient
    direction = gradient
    norm_now = inner_sum(residual, residual)
    for iteration in range(ITERS):
        product = hessian_times(direction)
        step_size = norm_now / inner_sum(direction, product)
        solution = tuple(
            (vector + step_size * update for vector, update in zip(solution, direction))
        )
        if iteration + 1 < ITERS:
            residual = tuple(
                (vector - step_size * update for vector, update in zip(residual, product))
            )
            norm_next = inner_sum(residual, residual)
            direction = tuple(
                (
                    vector + norm_next / norm_now * update
                    for vector, update in zip(residual, direction)
                )
            )
            norm_now = norm_next
    position_a = lax.axis_index(("ja", "ka")) * factor_a.shape[1]
    position_b = lax.axis_index(("ia", "ka")) * factor_b.shape[1]
    position_c = lax.axis_index(("ia", "ja")) * factor_c.shape[1]
    step_a = lax.dynamic_slice_in_dim(solution[0], position_a, factor_a.shape[1], 1)
    step_b = lax.dynamic_slice_in_dim(solution[1], position_b, factor_b.shape[1], 1)
    step_c = lax.dynamic_slice_in_dim(solution[2], position_c, factor_c.shape[1], 1)
    return (step_a, step_b, step_c)


def solution(mesh):
    placed = (
        P("ka", "ia", "ja"),
        P("ka", "ia", "ja"),
        P("ia", ("ja", "ka")),
        P("ja", ("ia", "ka")),
        P("ka", ("ia", "ja")),
    )
    return jax.shard_map(
        local,
        mesh=mesh,
        in_specs=placed,
        out_specs=(P("ia", ("ja", "ka")), P("ja", ("ia", "ka")), P("ka", ("ia", "ja"))),
        check_vma=False,
    )
```

profile of v0, /device:TPU:0, one launch (start us, length us, event | category | flops | bytes accessed | tf_op | source)
XLA Modules:
  0.0 519.4 jit_solution(12304898515846047202)
XLA Ops:
  7.2 14.5 %all_gather.10 = bf16[64,128]{0,1:T(8,128)(2,1)S(1)} all-gather(bf16[64,16]{0,1:T(8,128)(2,1)} %param.7), channel_id=1, replica_groups=mesh['ia'=4,'ja'=4,'ka'=2] {'ja','ka'}, dimensions={1}, use_global_device_ids=true | all-gather | bytes 18432 | tf_op jit(solution)/shard_map/all_gather | solution.py:19
  21.7 0.1 copy.21
  21.8 0.7 copy-done.3
  22.4 21.9 %all_gather.9 = bf16[32,128]{0,1:T(8,128)(2,1)S(1)} all-gather(bf16[32,8]{0,1:T(8,128)(2,1)S(1)} %copy-done.3), channel_id=1, replica_groups=mesh['ia'=4,'ja'=4,'ka'=2] {'ia','ja'}, dimensions={1}, use_global_device_ids=true | all-gather | bytes 8704 | tf_op jit(solution)/shard_map/all_gather | solution.py:21
  44.4 0.7 copy-done.2
  45.1 30.6 %all_gather.11 = bf16[128,128]{0,1:T(8,128)(2,1)S(1)} all-gather(bf16[128,16]{0,1:T(8,128)(2,1)S(1)} %copy-done.2), channel_id=1, replica_groups=mesh['ia'=4,'ja'=4,'ka'=2] {'ia','ka'}, dimensions={1}, use_global_device_ids=true | all-gather | bytes 36864 | tf_op jit(solution)/shard_map/all_gather | solution.py:20
  75.7 1.4 multiply_convert_fusion.1
  77.1 0.1 multiply_convert_fusion
  77.2 0.9 copy-done.1
  78.1 0.3 fusion.3
  78.4 1.0 fusion.16
  79.6 0.3 multiply_reduce_fusion.4
  80.0 0.1 multiply_reduce_fusion.5
  80.1 22.7 %psum.91 = f32[64,128]{1,0:T(8,128)S(1)} all-reduce(f32[64,128]{1,0:T(8,128)S(1)} %bitcast.75), channel_id=1, replica_groups=mesh['ia'=4,'ja'=4,'ka'=2] {'ja','ka'}, use_global_device_ids=true, to_apply=%region_0.0 | all-reduce | flops 8192 | bytes 65536 | tf_op jit(solution)/shard_map/psum | solution.py:45
  102.8 58.1 %psum.93 = f32[32,128]{1,0:T(8,128)S(1)} all-reduce(f32[32,128]{1,0:T(8,128)S(1)} %bitcast.78), channel_id=1, replica_groups=mesh['ia'=4,'ja'=4,'ka'=2] {'ia','ja'}, use_global_device_ids=true, to_apply=%region_4.0 | all-reduce | flops 4096 | bytes 32768 | tf_op jit(solution)/shard_map/psum | solution.py:47
  160.8 0.2 add_convert_fusion.1
  161.0 1.1 fusion.12
  162.2 0.3 fusion.4
  162.5 1.0 fusion.17
  163.4 0.3 multiply_reduce_fusion.2
  163.8 0.1 multiply_reduce_fusion.3
  164.0 23.9 %psum.95 = f32[64,128]{1,0:T(8,128)S(1)} all-reduce(f32[64,128]{1,0:T(8,128)S(1)} %bitcast.76), channel_id=1, replica_groups=mesh['ia'=4,'ja'=4,'ka'=2] {'ja','ka'}, use_global_device_ids=true, to_apply=%region_7.0 | all-reduce | flops 8192 | bytes 65536 | tf_op jit(solution)/shard_map/psum | solution.py:45
  187.8 0.6 multiply_reduce_fusion.10
  188.4 57.7 %psum.97 = f32[32,128]{1,0:T(8,128)S(1)} all-reduce(f32[32,128]{1,0:T(8,128)S(1)} %bitcast.77), channel_id=1, replica_groups=mesh['ia'=4,'ja'=4,'ka'=2] {'ia','ja'}, use_global_device_ids=true, to_apply=%region_11.0 | all-reduce | flops 4096 | bytes 32768 | tf_op jit(solution)/shard_map/psum | solution.py:47
  246.2 0.7 multiply_reduce_fusion.13
  248.1 1.5 multiply_reduce_fusion.7
  252.3 36.9 %all-reduce = (f32[]{:T(128)}, f32[]{:T(128)}) all-reduce(f32[]{:T(128)S(6)} %add.125, f32[]{:T(128)S(6)} %add.132), channel_id=1, replica_groups=mesh['ia'=4,'ja'=4,'ka'=2] {'ia','ja','ka'}, use_global_device_ids=true, to_apply=%region_6.0 | all-reduce | flops 2 | bytes 16 | tf_op jit(solution)/shard_map/psum | solution.py:63
  290.5 0.6 multiply_reduce_fusion.12
  291.8 0.6 multiply_reduce_fusion.9
  292.4 0.6 multiply_reduce_fusion.6
  294.3 41.9 %psum.99 = f32[]{:T(128)} all-reduce(f32[]{:T(128)S(6)} %add.134), channel_id=1, replica_groups=mesh['ia'=4,'ja'=4,'ka'=2] {'ia','ja','ka'}, use_global_device_ids=true, to_apply=%region_17.0 | all-reduce | flops 1 | bytes 8 | tf_op jit(solution)/shard_map/psum | solution.py:63
  337.6 0.3 fusion.10
  337.9 0.2 add_convert_fusion
  338.1 0.3 fusion.5
  338.4 0.3 multiply_reduce_fusion
  338.7 1.0 fusion.18
  339.6 59.3 %psum.102 = f32[32,128]{1,0:T(8,128)S(1)} all-reduce(f32[32,128]{1,0:T(8,128)S(1)} %bitcast.79), channel_id=1, replica_groups=mesh['ia'=4,'ja'=4,'ka'=2] {'ia','ja'}, use_global_device_ids=true, to_apply=%region_22.0 | all-reduce | flops 4096 | bytes 32768 | tf_op jit(solution)/shard_map/psum | solution.py:47
  398.9 0.6 fusion.14
  400.2 0.1 multiply_reduce_fusion.1
  400.3 23.2 %psum.100 = f32[64,128]{1,0:T(8,128)S(1)} all-reduce(f32[64,128]{1,0:T(8,128)S(1)} %bitcast.74), channel_id=1, replica_groups=mesh['ia'=4,'ja'=4,'ka'=2] {'ja','ka'}, use_global_device_ids=true, to_apply=%region_18.0 | all-reduce | flops 8192 | bytes 65536 | tf_op jit(solution)/shard_map/psum | solution.py:45
  423.5 0.6 fusion.8
  424.1 42.1 %all-reduce.9.cloned.1.call-done = f32[128,128]{1,0:T(8,128)} async-done(((f32[128,128]{1,0:T(8,128)}), f32[128,128]{1,0:T(8,128)}) %all-reduce.9.cloned.1.call-update) | async-done | bytes 65552 | tf_op jit(solution)/shard_map/psum | solution.py:46
  466.2 1.5 fusion.6
  469.0 40.3 %psum.103 = f32[]{:T(128)} all-reduce(f32[]{:T(128)S(6)} %add.144), channel_id=1, replica_groups=mesh['ia'=4,'ja'=4,'ka'=2] {'ia','ja','ka'}, use_global_device_ids=true, to_apply=%region_24.0 | all-reduce | flops 1 | bytes 8 | tf_op jit(solution)/shard_map/psum | solution.py:63
  510.7 0.7 copy.24
  511.4 0.1 fusion.7
  511.5 0.7 copy.23
  512.2 0.7 copy.22
  (27 shorter events, 0.7 us)
Async XLA Ops:
  7.2 153.9 %all-reduce.5.cloned.1.call-start = ((), (), s32[]{:S(2)}) async-start(), calls=%async_computation | async-start | bytes 131072 | tf_op jit(solution)/shard_map/psum | solution.py:46
  21.8 0.7 copy-start.3
  44.4 0.7 copy-start.2
  77.0 1.0 copy-start.1
  79.4 168.7 %all-reduce.7.cloned.1.call-start = ((), (), s32[]{:S(2)}) async-start(), calls=%async_computation.1 | async-start | bytes 131072 | tf_op jit(solution)/shard_map/psum | solution.py:46
  163.8 302.5 %all-reduce.9.cloned.1.call-start = ((), (), s32[]{:S(2)}) async-start(), calls=%async_computation.2 | async-start | bytes 131072 | tf_op jit(solution)/shard_map/psum | solution.py:46
  188.4 59.7 %copy-start = (f32[128,128]{1,0:T(8,128)S(1)}, f32[128,128]{1,0:T(8,128)}, u32[]{:S(2)}) copy-start(f32[128,128]{1,0:T(8,128)} %all-reduce.5.cloned.1.call-done) | copy-start | bytes 196612
Sparse Core Ops, SparseCore 0:
  79.5 66.1 all-reduce.4
  163.9 66.5 all-reduce.6
  400.3 65.8 all-reduce.8
where the time goes:
time: 520 us; the launch traced here: 519 us
  blocking collectives  431 us (83%)
  waiting for transfers between devices  42.2 us (8%)
  between operations  25.8 us (5%)
  other arithmetic  9.88 us (2%)
  matrix products  6.15 us (1%)
    psum x3, blocking collectives, settle(): total_c = lax.psum(parts[2], ('ia', 'ja'))  175 us
    psum x3, blocking collectives, inner_sum(): return lax.psum(local_sum, ('ia', 'ja', 'ka'))  119 us
    psum x3, blocking collectives, settle(): total_a = lax.psum(parts[0], ('ja', 'ka'))  69.7 us
    psum x3, waiting for transfers between devices, settle(): total_b = lax.psum(parts[1], ('ia', 'ka'))  42.1 us
    all_gather x1, blocking collectives, local(): full_b = lax.all_gather(factor_b, ('ia', 'ka'), axis=1, tiled=True)  30.6 us
    all_gather x1, blocking collectives, local(): full_c = lax.all_gather(factor_c, ('ia', 'ja'), axis=1, tiled=True)  21.9 us
    all_gather x1, blocking collectives, local(): full_a = lax.all_gather(factor_a, ('ja', 'ka'), axis=1, tiled=True)  14.5 us
  transfers between devices with their start and end apart: 3, of which 1 were waited for; matrix products, arithmetic and copies ran while one was open for 1% of the time, Pallas kernels for 0%

commit v1 on v0

--- a/solution.py
+++ b/solution.py
@@ -60,7 +60,7 @@
                 for left_side, right_side, factor in zip(first, second, scales)
             )
         )
-        return lax.psum(local_sum, ("ia", "ja", "ka"))
+        return lax.psum(lax.psum(local_sum, "ia"), ("ja", "ka"))
 
     def expand(direction):
         hat_a = direction[0].astype(jnp.bfloat16)

time: 520 us -> 472 us (0.908)
  blocking collectives: 431 us -> 382 us
    psum x3 -> x6, blocking collectives: 119 us -> 72.3 us  [inner_sum(): return lax.psum(lax.psum(local_sum, 'ia'), ('ja', 'ka'))]
where the time goes in v1:
time: 472 us; the launch traced here: 471 us
  blocking collectives  382 us (81%)
  waiting for transfers between devices  42.2 us (9%)
  between operations  25.8 us (5%)
  other arithmetic  9.88 us (2%)
  matrix products  6.16 us (1%)
    psum x3, blocking collectives, settle(): total_c = lax.psum(parts[2], ('ia', 'ja'))  173 us
    psum x6, blocking collectives, inner_sum(): return lax.psum(lax.psum(local_sum, 'ia'), ('ja', 'ka'))  72.3 us
    psum x3, blocking collectives, settle(): total_a = lax.psum(parts[0], ('ja', 'ka'))  69.7 us
    psum x3, waiting for transfers between devices, settle(): total_b = lax.psum(parts[1], ('ia', 'ka'))  42.1 us
    all_gather x1, blocking collectives, local(): full_b = lax.all_gather(factor_b, ('ia', 'ka'), axis=1, tiled=True)  30.6 us
    all_gather x1, blocking collectives, local(): full_c = lax.all_gather(factor_c, ('ia', 'ja'), axis=1, tiled=True)  21.9 us
    all_gather x1, blocking collectives, local(): full_a = lax.all_gather(factor_a, ('ja', 'ka'), axis=1, tiled=True)  14.5 us
  transfers between devices with their start and end apart: 3, of which 1 were waited for; matrix products, arithmetic and copies ran while one was open for 1% of the time, Pallas kernels for 0%

profile of v1, /device:TPU:0, one launch (start us, length us, event | category | flops | bytes accessed | tf_op | source)
XLA Modules:
  0.0 471.0 jit_solution(3898853795339588339)
XLA Ops:
  7.2 14.5 %all_gather.10 = bf16[64,128]{0,1:T(8,128)(2,1)S(1)} all-gather(bf16[64,16]{0,1:T(8,128)(2,1)} %param.7), channel_id=1, replica_groups=mesh['ia'=4,'ja'=4,'ka'=2] {'ja','ka'}, dimensions={1}, use_global_device_ids=true | all-gather | bytes 18432 | tf_op jit(solution)/shard_map/all_gather | solution.py:19
  21.8 0.7 copy-done.3
  22.4 21.9 %all_gather.9 = bf16[32,128]{0,1:T(8,128)(2,1)S(1)} all-gather(bf16[32,8]{0,1:T(8,128)(2,1)S(1)} %copy-done.3), channel_id=1, replica_groups=mesh['ia'=4,'ja'=4,'ka'=2] {'ia','ja'}, dimensions={1}, use_global_device_ids=true | all-gather | bytes 8704 | tf_op jit(solution)/shard_map/all_gather | solution.py:21
  44.4 0.7 copy-done.2
  45.1 30.6 %all_gather.11 = bf16[128,128]{0,1:T(8,128)(2,1)S(1)} all-gather(bf16[128,16]{0,1:T(8,128)(2,1)S(1)} %copy-done.2), channel_id=1, replica_groups=mesh['ia'=4,'ja'=4,'ka'=2] {'ia','ka'}, dimensions={1}, use_global_device_ids=true | all-gather | bytes 36864 | tf_op jit(solution)/shard_map/all_gather | solution.py:20
  75.7 1.4 multiply_convert_fusion.1
  77.2 0.9 copy-done.1
  78.1 0.3 fusion.3
  78.4 1.0 fusion.16
  79.6 0.3 multiply_reduce_fusion.4
  80.0 0.1 multiply_reduce_fusion.5
  80.1 22.7 %psum.119 = f32[64,128]{1,0:T(8,128)S(1)} all-reduce(f32[64,128]{1,0:T(8,128)S(1)} %bitcast.75), channel_id=1, replica_groups=mesh['ia'=4,'ja'=4,'ka'=2] {'ja','ka'}, use_global_device_ids=true, to_apply=%region_0.0 | all-reduce | flops 8192 | bytes 65536 | tf_op jit(solution)/shard_map/psum | solution.py:45
  102.8 58.1 %psum.121 = f32[32,128]{1,0:T(8,128)S(1)} all-reduce(f32[32,128]{1,0:T(8,128)S(1)} %bitcast.78), channel_id=1, replica_groups=mesh['ia'=4,'ja'=4,'ka'=2] {'ia','ja'}, use_global_device_ids=true, to_apply=%region_4.0 | all-reduce | flops 4096 | bytes 32768 | tf_op jit(solution)/shard_map/psum | solution.py:47
  160.8 0.2 add_convert_fusion.1
  161.0 1.1 fusion.12
  162.2 0.3 fusion.4
  162.5 1.0 fusion.17
  163.4 0.3 multiply_reduce_fusion.2
  163.8 0.1 multiply_reduce_fusion.3
  164.0 23.9 %psum.124 = f32[64,128]{1,0:T(8,128)S(1)} all-reduce(f32[64,128]{1,0:T(8,128)S(1)} %bitcast.76), channel_id=1, replica_groups=mesh['ia'=4,'ja'=4,'ka'=2] {'ja','ka'}, use_global_device_ids=true, to_apply=%region_8.0 | all-reduce | flops 8192 | bytes 65536 | tf_op jit(solution)/shard_map/psum | solution.py:45
  187.8 0.6 multiply_reduce_fusion.10
  188.4 57.7 %psum.126 = f32[32,128]{1,0:T(8,128)S(1)} all-reduce(f32[32,128]{1,0:T(8,128)S(1)} %bitcast.77), channel_id=1, replica_groups=mesh['ia'=4,'ja'=4,'ka'=2] {'ia','ja'}, use_global_device_ids=true, to_apply=%region_12.0 | all-reduce | flops 4096 | bytes 32768 | tf_op jit(solution)/shard_map/psum | solution.py:47
  246.2 0.7 multiply_reduce_fusion.13
  248.1 1.5 multiply_reduce_fusion.7
  252.3 8.9 %all-reduce.1 = (f32[]{:T(128)}, f32[]{:T(128)}) all-reduce(f32[]{:T(128)S(6)} %add.133, f32[]{:T(128)S(6)} %add.140), channel_id=1, replica_groups=mesh['ia'=4,'ja'=4,'ka'=2] {'ia'}, use_global_device_ids=true, to_apply=%region_6.0 | all-reduce | flops 2 | bytes 16 | tf_op jit(solution)/shard_map/psum | solution.py:63
  261.2 13.4 %all-reduce = (f32[]{:T(128)}, f32[]{:T(128)}) all-reduce(f32[]{:T(128)} %get-tuple-element.20, f32[]{:T(128)} %get-tuple-element.21), channel_id=1, replica_groups=mesh['ia'=4,'ja'=4,'ka'=2] {'ja','ka'}, use_global_device_ids=true, to_apply=%region_7.0 | all-reduce | flops 2 | bytes 16 | tf_op jit(solution)/shard_map/psum | solution.py:63
  275.9 0.6 multiply_reduce_fusion.12
  277.2 0.6 multiply_reduce_fusion.9
  277.8 0.6 multiply_reduce_fusion.6
  279.7 10.9 %psum.129 = f32[]{:T(128)} all-reduce(f32[]{:T(128)S(6)} %add.142), channel_id=1, replica_groups=mesh['ia'=4,'ja'=4,'ka'=2] {'ia'}, use_global_device_ids=true, to_apply=%region_19.0 | all-reduce | flops 1 | bytes 8 | tf_op jit(solution)/shard_map/psum | solution.py:63
  290.6 13.9 %psum.130 = f32[]{:T(128)} all-reduce(f32[]{:T(128)} %psum.129), channel_id=1, replica_groups=mesh['ia'=4,'ja'=4,'ka'=2] {'ja','ka'}, use_global_device_ids=true, to_apply=%region_20.0 | all-reduce | flops 1 | bytes 8 | tf_op jit(solution)/shard_map/psum | solution.py:63
  305.9 0.3 fusion.10
  306.2 0.2 add_convert_fusion
  306.3 0.3 fusion.5
  306.6 0.3 multiply_reduce_fusion
  306.9 1.0 fusion.18
  307.9 57.6 %psum.133 = f32[32,128]{1,0:T(8,128)S(1)} all-reduce(f32[32,128]{1,0:T(8,128)S(1)} %bitcast.79), channel_id=1, replica_groups=mesh['ia'=4,'ja'=4,'ka'=2] {'ia','ja'}, use_global_device_ids=true, to_apply=%region_25.0 | all-reduce | flops 4096 | bytes 32768 | tf_op jit(solution)/shard_map/psum | solution.py:47
  365.5 0.6 fusion.14
  366.8 0.1 multiply_reduce_fusion.1
  366.9 23.2 %psum.131 = f32[64,128]{1,0:T(8,128)S(1)} all-reduce(f32[64,128]{1,0:T(8,128)S(1)} %bitcast.74), channel_id=1, replica_groups=mesh['ia'=4,'ja'=4,'ka'=2] {'ja','ka'}, use_global_device_ids=true, to_apply=%region_21.0 | all-reduce | flops 8192 | bytes 65536 | tf_op jit(solution)/shard_map/psum | solution.py:45
  390.1 0.6 fusion.8
  390.8 42.1 %all-reduce.10.cloned.1.call-done = f32[128,128]{1,0:T(8,128)} async-done(((f32[128,128]{1,0:T(8,128)}), f32[128,128]{1,0:T(8,128)}) %all-reduce.10.cloned.1.call-update) | async-done | bytes 65552 | tf_op jit(solution)/shard_map/psum | solution.py:46
  432.9 1.5 fusion.6
  435.6 11.2 %psum.134 = f32[]{:T(128)} all-reduce(f32[]{:T(128)S(6)} %add.152), channel_id=1, replica_groups=mesh['ia'=4,'ja'=4,'ka'=2] {'ia'}, use_global_device_ids=true, to_apply=%region_27.0 | all-reduce | flops 1 | bytes 8 | tf_op jit(solution)/shard_map/psum | solution.py:63
  446.9 14.0 %psum.135 = f32[]{:T(128)} all-reduce(f32[]{:T(128)} %psum.134), channel_id=1, replica_groups=mesh['ia'=4,'ja'=4,'ka'=2] {'ja','ka'}, use_global_device_ids=true, to_apply=%region_28.0 | all-reduce | flops 1 | bytes 8 | tf_op jit(solution)/shard_map/psum | solution.py:63
  462.3 0.7 copy.24
  463.1 0.7 copy.23
  463.8 0.7 copy.22
  (30 shorter events, 1.0 us)
Async XLA Ops:
  7.2 153.9 %all-reduce.6.cloned.1.call-start = ((), (), s32[]{:S(2)}) async-start(), calls=%async_computation | async-start | bytes 131072 | tf_op jit(solution)/shard_map/psum | solution.py:46
  21.8 0.7 copy-start.3
  44.4 0.7 copy-start.2
  77.0 1.0 copy-start.1
  79.4 168.7 %all-reduce.8.cloned.1.call-start = ((), (), s32[]{:S(2)}) async-start(), calls=%async_computation.1 | async-start | bytes 131072 | tf_op jit(solution)/shard_map/psum | solution.py:46
  163.8 269.1 %all-reduce.10.cloned.1.call-start = ((), (), s32[]{:S(2)}) async-start(), calls=%async_computation.2 | async-start | bytes 131072 | tf_op jit(solution)/shard_map/psum | solution.py:46
  188.4 59.7 %copy-start = (f32[128,128]{1,0:T(8,128)S(1)}, f32[128,128]{1,0:T(8,128)}, u32[]{:S(2)}) copy-start(f32[128,128]{1,0:T(8,128)} %all-reduce.6.cloned.1.call-done) | copy-start | bytes 196612
Sparse Core Ops, SparseCore 0:
  79.5 66.1 all-reduce.5
  163.9 66.5 all-reduce.7
  366.9 65.9 all-reduce.9
